TPU v7x, 32 devices: a whole 2x2x4 slice. The times are simulated.
32 devices in a mesh: dp: 4 (over y, x), row: 2 (over core), col: 4 (over z).
Axes of the slice: x: 2, y: 2, z: 4, core: 2. Of those that a mesh axis runs over, the one named last changes fastest.
Arguments:
- states: bfloat16 [25088, 1024], P(('dp', 'row', 'col')), may hold values from -6 to 6
- ln1_gain: bfloat16 [1024], P('row'), may hold values from 0.5 to 1.5
- ln1_bias: bfloat16 [1024], P('row'), may hold values from -0.59765625 to 0.59765625
- w_qkv: bfloat16 [1024, 3, 1024], P('row', None, 'col'), may hold values from -0.1875 to 0.1875
- q_bias: bfloat16 [1024], P('col'), may hold values from -1.796875 to 1.796875
- v_bias: bfloat16 [1024], P('col'), may hold values from -0.29882812 to 0.29882812
- w_proj: bfloat16 [1024, 1024], P('col', 'row'), may hold values from -0.75 to 0.75
- proj_bias: bfloat16 [1024], P('row'), may hold values from -0.59765625 to 0.59765625
- ln2_gain: bfloat16 [1024], P('row'), may hold values from 0.5 to 1.5
- ln2_bias: bfloat16 [1024], P('row'), may hold values from -0.59765625 to 0.59765625
- w_fc1: bfloat16 [1024, 4096], P('row', 'col'), may hold values from -0.1875 to 0.1875
- fc1_bias: bfloat16 [4096], P('col'), may hold values from -0.59765625 to 0.59765625
- w_fc2: bfloat16 [4096, 1024], P('col', 'row'), may hold values from -0.09375 to 0.09375
- fc2_bias: bfloat16 [1024], P('row'), may hold values from -0.59765625 to 0.59765625
- teacher: bfloat16 [25088, 1024], P(('dp', 'row', 'col')), may hold values from -6 to 6
- loss_mask: int32 [25088], replicated, may hold values 0 or 1
- lengths: int32 [16], replicated, may hold values from 784 to 1568, as said below
Outputs:
- states_out: bfloat16 [25088, 1024], P(('dp', 'row', 'col'))
- loss: float32 [], replicated
- grad_states: bfloat16 [25088, 1024], P(('dp', 'row', 'col'))
- grad_ln1_gain: float32 [1024], P('row')
- grad_ln1_bias: float32 [1024], P('row')
- grad_w_qkv: float32 [1024, 3, 1024], P('row', None, 'col')
- grad_q_bias: float32 [1024], P('col')
- grad_v_bias: float32 [1024], P('col')
- grad_w_proj: float32 [1024, 1024], P('col', 'row')
- grad_proj_bias: float32 [1024], P('row')
- grad_ln2_gain: float32 [1024], P('row')
- grad_ln2_bias: float32 [1024], P('row')
- grad_w_fc1: float32 [1024, 4096], P('row', 'col')
- grad_fc1_bias: float32 [4096], P('col')
- grad_w_fc2: float32 [4096, 1024], P('col', 'row')
- grad_fc2_bias: float32 [1024], P('row')
Inputs may be any that keep to these rules, and one draw needn't show every extreme that they name: `lengths`: each entry is the number of real tube tokens of one clip, from 784 to 1568; some clip has all 1568. Positions at or beyond it are padding.
All inputs are finite; a program needn't handle non-finite values.
Results may differ from a plain program's by a relative error of at most 0.012.
The roundings to bfloat16 on the way count: a program that leaves them out, or rounds other values in their place, can miss the bound.
Values may be sent and summed in bfloat16 or wider, within the bound.
No kernel may reach another device: no remote copies, remote signals or barrier semaphores. Data moves between devices by JAX's collectives and lax.ppermute only.
A program may use at most 320 MiB of HBM per device.

v0:
```python
import jax
import jax.numpy as jnp
from jax import lax
from jax.sharding import PartitionSpec as P

HD = 64
L = 1568
EPSILON = 1e-06
MASKED = -1e30
ROOT_HALF = 0.7071067811865476
DENSITY_FACTOR = 0.3989422804014327


def normalize(values, factor, offset):
    centered = values - jnp.mean(values, axis=-1, keepdims=True)
    spread = lax.rsqrt(jnp.mean(centered * centered, axis=-1, keepdims=True) + EPSILON)
    normal = centered * spread
    return (normal * factor + offset, normal, spread)


def norm_back(upstream, normal, spread, factor):
    inner = upstream * factor
    center_term = jnp.mean(inner, axis=-1, keepdims=True)
    slope_term = jnp.mean(inner * normal, axis=-1, keepdims=True)
    back = spread * (inner - center_term - normal * slope_term)
    return (back, jnp.sum(upstream * normal, axis=0), jnp.sum(upstream, axis=0))


def gelu_value(values):
    return values * (0.5 * (1.0 + lax.erf(values * ROOT_HALF)))


def gelu_slope(values):
    normal_cdf = 0.5 * (1.0 + lax.erf(values * ROOT_HALF))
    return normal_cdf + values * jnp.exp(-0.5 * values * values) * DENSITY_FACTOR


def masked_scores(queries, key_rows, length, score_scale):
    logits = (
        jnp.einsum("ihd,jhd->hij", queries, key_rows, preferred_element_type=jnp.float32)
        * score_scale
    )
    keep = jnp.arange(key_rows.shape[0]) < length
    return jnp.where(keep[None, None, :], logits, MASKED)


def attend_clip(packed, length, score_scale):
    half_span = packed.shape[0] // 2
    key_rows = packed[:, 1]
    value_rows = packed[:, 2]
    pieces = []
    totals = []
    for block_index in range(2):
        queries = packed[block_index * half_span : (block_index + 1) * half_span, 0]
        logits = masked_scores(queries, key_rows, length, score_scale)
        peak = jnp.max(logits, axis=-1, keepdims=True)
        total = peak + jnp.log(jnp.sum(jnp.exp(logits - peak), axis=-1, keepdims=True))
        weights = jnp.exp(logits - total).astype(jnp.bfloat16)
        pieces.append(
            jnp.einsum("hij,jhd->ihd", weights, value_rows, preferred_element_type=jnp.float32)
        )
        totals.append(total[..., 0])
    return (jnp.concatenate(pieces, 0), jnp.concatenate(totals, 1))


def attend_clip_back(packed, length, totals, upstream, score_scale):
    half_span = packed.shape[0] // 2
    key_rows = packed[:, 1]
    value_rows = packed[:, 2]
    grad_keys = jnp.zeros(key_rows.shape, jnp.float32)
    grad_values = jnp.zeros(value_rows.shape, jnp.float32)
    grad_queries = []
    for block_index in range(2):
        first = block_index * half_span
        queries = packed[first : first + half_span, 0]
        logits = masked_scores(queries, key_rows, length, score_scale)
        probs = jnp.exp(logits - totals[:, first : first + half_span][..., None])
        incoming = upstream[first : first + half_span]
        grad_values = grad_values + jnp.einsum(
            "hij,ihd->jhd", probs.astype(jnp.bfloat16), incoming, preferred_element_type=jnp.float32
        )
        grad_probs = jnp.einsum(
            "ihd,jhd->hij", incoming, value_rows, preferred_element_type=jnp.float32
        )
        grad_logits = (
            probs * (grad_probs - jnp.sum(probs * grad_probs, axis=-1, keepdims=True))
        ).astype(jnp.bfloat16)
        grad_queries.append(
            jnp.einsum("hij,jhd->ihd", grad_logits, key_rows, preferred_element_type=jnp.float32)
            * score_scale
        )
        grad_keys = (
            grad_keys
            + jnp.einsum("hij,ihd->jhd", grad_logits, queries, preferred_element_type=jnp.float32)
            * score_scale
        )
    return jnp.stack([jnp.concatenate(grad_queries, 0), grad_keys, grad_values], axis=1)


def local(
    states,
    ln1_gain,
    ln1_bias,
    w_qkv,
    q_bias,
    v_bias,
    w_proj,
    proj_bias,
    ln2_gain,
    ln2_bias,
    w_fc1,
    fc1_bias,
    w_fc2,
    fc2_bias,
    teacher,
    loss_mask,
    lengths,
):
    row_count = lax.axis_size("row")
    col_count = lax.axis_size("col")
    col_index = lax.axis_index("col")
    group_index = lax.axis_index("dp") * row_count + lax.axis_index("row")
    local_rows = states.shape[0]
    width = states.shape[1]
    group_rows = local_rows * col_count
    clip_count = group_rows // L
    head_width = w_qkv.shape[2]
    heads_here = head_width // HD
    hidden_width = w_fc1.shape[1]
    score_scale = HD ** (-0.5)
    vectors = jnp.stack([ln1_gain, ln1_bias, proj_bias, ln2_gain, ln2_bias, fc2_bias])
    qkv_full, proj_full, fc1_full, fc2_full, vector_full = (
        lax.all_gather(w_qkv, "row", axis=0, tiled=True),
        lax.all_gather(w_proj, "row", axis=1, tiled=True),
        lax.all_gather(w_fc1, "row", axis=0, tiled=True),
        lax.all_gather(w_fc2, "row", axis=1, tiled=True),
        lax.all_gather(vectors, "row", axis=1, tiled=True),
    )
    vector_full = vector_full.astype(jnp.float32)
    gain_one = vector_full[0]
    shift_one = vector_full[1]
    bias_proj = vector_full[2]
    gain_two = vector_full[3]
    shift_two = vector_full[4]
    bias_two = vector_full[5]
    all_clips = lengths.shape[0]
    valid_all = (
        loss_mask.reshape(all_clips, L) * (jnp.arange(L)[None, :] < lengths[:, None])
    ).astype(jnp.float32)
    valid_total = jnp.maximum(jnp.sum(valid_all), 1.0)
    first_row = (group_index * col_count + col_index) * local_rows
    valid = lax.dynamic_slice_in_dim(valid_all.reshape(all_clips * L), first_row, local_rows)
    my_lengths = lax.dynamic_slice_in_dim(lengths, group_index * clip_count, clip_count)
    inputs = states.astype(jnp.float32)
    norm_one, unit_one, spread_one = normalize(inputs, gain_one, shift_one)
    norm_one = norm_one.astype(jnp.bfloat16)
    tokens_one = lax.all_gather(norm_one, "col", axis=0, tiled=True)
    qkv_matrix = qkv_full.reshape(width, 3 * head_width)
    projected = jnp.dot(tokens_one, qkv_matrix, preferred_element_type=jnp.float32).reshape(
        group_rows, 3, head_width
    )
    bias_rows = jnp.stack(
        [
            q_bias.astype(jnp.float32),
            jnp.zeros((head_width,), jnp.float32),
            v_bias.astype(jnp.float32),
        ]
    )
    packed = (projected + bias_rows[None]).astype(jnp.bfloat16)
    clips_packed = packed.reshape(clip_count, L, 3, heads_here, HD)
    attended, totals = lax.map(
        lambda element: attend_clip(element[0], element[1], score_scale), (clips_packed, my_lengths)
    )
    attended = attended.reshape(group_rows, head_width).astype(jnp.bfloat16)
    proj_whole, qkv_whole = (
        lax.all_gather(proj_full, "col", axis=0, tiled=True),
        lax.all_gather(qkv_full, "col", axis=2, tiled=True),
    )
    attended_rows = lax.all_to_all(attended, "col", split_axis=0, concat_axis=1, tiled=True)
    middle = inputs + (
        jnp.dot(attended_rows, proj_whole, preferred_element_type=jnp.float32) + bias_proj
    )
    norm_two, unit_two, spread_two = normalize(middle, gain_two, shift_two)
    norm_two = norm_two.astype(jnp.bfloat16)
    fc1_whole, fc2_whole, fc1_bias_whole = (
        lax.all_gather(fc1_full, "col", axis=1, tiled=True),
        lax.all_gather(fc2_full, "col", axis=0, tiled=True),
        lax.all_gather(fc1_bias, "col", axis=0, tiled=True),
    )
    hidden_pre = jnp.dot(
        norm_two, fc1_whole, preferred_element_type=jnp.float32
    ) + fc1_bias_whole.astype(jnp.float32)
    hidden = gelu_value(hidden_pre).astype(jnp.bfloat16)
    outputs = middle + (jnp.dot(hidden, fc2_whole, preferred_element_type=jnp.float32) + bias_two)
    differ = outputs - teacher.astype(jnp.float32)
    numerator = jnp.sum(valid[:, None] * differ * differ)
    loss_scale = all_clips * L * width / 2.0
    grad_out = loss_scale * 2.0 / (valid_total * width) * valid[:, None] * differ
    grad_low = grad_out.astype(jnp.bfloat16)
    grad_hidden = jnp.dot(grad_low, fc2_whole.T, preferred_element_type=jnp.float32)
    grad_pre = (grad_hidden * gelu_slope(hidden_pre)).astype(jnp.bfloat16)
    wide_fc2 = jnp.dot(hidden.T, grad_low, preferred_element_type=jnp.float32)
    wide_fc1 = jnp.dot(norm_two.T, grad_pre, preferred_element_type=jnp.float32)
    fc1_grad_part, fc2_grad_part = (
        lax.psum_scatter(
            wide_fc1.astype(jnp.bfloat16), "col", scatter_dimension=1, tiled=True
        ).astype(jnp.float32),
        lax.psum_scatter(
            wide_fc2.astype(jnp.bfloat16), "col", scatter_dimension=0, tiled=True
        ).astype(jnp.float32),
    )
    fc1_bias_sum = jnp.sum(grad_pre, axis=0, dtype=jnp.float32)
    grad_norm_two = jnp.dot(grad_pre, fc1_whole.T, preferred_element_type=jnp.float32)
    back_two, gain_two_grad, shift_two_grad = norm_back(
        grad_norm_two, unit_two, spread_two, gain_two
    )
    grad_mid = grad_out + back_two
    mid_low = grad_mid.astype(jnp.bfloat16)
    wide_proj = jnp.dot(attended_rows.T, mid_low, preferred_element_type=jnp.float32)
    proj_grad_part = lax.psum_scatter(
        wide_proj.astype(jnp.bfloat16), "col", scatter_dimension=0, tiled=True
    )
    grad_attended_rows = jnp.dot(mid_low, proj_whole.T, preferred_element_type=jnp.float32).astype(
        jnp.bfloat16
    )
    grad_attended = lax.all_to_all(
        grad_attended_rows, "col", split_axis=1, concat_axis=0, tiled=True
    )
    grads_packed = lax.map(
        lambda element: attend_clip_back(
            element[0], element[1], element[2], element[3], score_scale
        ),
        (clips_packed, my_lengths, totals, grad_attended.reshape(clip_count, L, heads_here, HD)),
    )
    grads_packed = grads_packed.reshape(group_rows, 3 * head_width).astype(jnp.bfloat16)
    qkv_grad_part = jnp.dot(tokens_one.T, grads_packed, preferred_element_type=jnp.float32).reshape(
        width, 3, head_width
    )
    bias_sums = jnp.sum(grads_packed.reshape(group_rows, 3, head_width), axis=0, dtype=jnp.float32)
    grads_rows = lax.all_to_all(
        grads_packed.reshape(group_rows, 3, head_width),
        "col",
        split_axis=0,
        concat_axis=2,
        tiled=True,
    )
    grad_norm_one = jnp.dot(
        grads_rows.reshape(local_rows, 3 * width),
        qkv_whole.reshape(width, 3 * width).T,
        preferred_element_type=jnp.float32,
    )
    back_one, gain_one_grad, shift_one_grad = norm_back(
        grad_norm_one, unit_one, spread_one, gain_one
    )
    grad_states = (grad_mid + back_one).astype(jnp.bfloat16)
    proj_bias_grad = jnp.sum(mid_low, axis=0, dtype=jnp.float32)
    fc2_bias_grad = jnp.sum(grad_low, axis=0, dtype=jnp.float32)
    token_vectors = jnp.stack(
        [
            gain_one_grad,
            shift_one_grad,
            proj_bias_grad,
            gain_two_grad,
            shift_two_grad,
            fc2_bias_grad,
        ]
    )
    head_vectors = lax.dynamic_update_slice(
        jnp.zeros((2, width), jnp.float32),
        jnp.stack([bias_sums[0], bias_sums[2]]),
        (0, col_index * head_width),
    )
    token_sums, head_sums, fc1_sums, loss_sum = lax.psum(
        (token_vectors, head_vectors, fc1_bias_sum, numerator), ("dp", "row", "col")
    )
    qkv_rows, proj_cols, fc1_rows, fc2_cols = (
        lax.psum_scatter(
            qkv_grad_part.astype(jnp.bfloat16), "row", scatter_dimension=0, tiled=True
        ).astype(jnp.float32),
        lax.psum_scatter(proj_grad_part, "row", scatter_dimension=1, tiled=True).astype(
            jnp.float32
        ),
        lax.psum_scatter(
            fc1_grad_part.astype(jnp.bfloat16), "row", scatter_dimension=0, tiled=True
        ).astype(jnp.float32),
        lax.psum_scatter(
            fc2_grad_part.astype(jnp.bfloat16), "row", scatter_dimension=1, tiled=True
        ).astype(jnp.float32),
    )
    qkv_grad, proj_grad, fc1_grad, fc2_grad = (
        lax.psum(qkv_rows.astype(jnp.bfloat16), "dp").astype(jnp.float32),
        lax.psum(proj_cols.astype(jnp.bfloat16), "dp").astype(jnp.float32),
        lax.psum(fc1_rows.astype(jnp.bfloat16), "dp").astype(jnp.float32),
        lax.psum(fc2_cols.astype(jnp.bfloat16), "dp").astype(jnp.float32),
    )
    half_width = width // row_count
    token_part = lax.dynamic_slice_in_dim(
        token_sums, lax.axis_index("row") * half_width, half_width, 1
    )
    head_part = lax.dynamic_slice_in_dim(head_sums, col_index * head_width, head_width, 1)
    fc1_part = lax.dynamic_slice_in_dim(fc1_sums, col_index * hidden_width, hidden_width, 0)
    loss_value = loss_sum / (valid_total * width)
    return (
        outputs.astype(jnp.bfloat16),
        loss_value,
        grad_states,
        token_part[0],
        token_part[1],
        qkv_grad,
        head_part[0],
        head_part[1],
        proj_grad,
        token_part[2],
        token_part[3],
        token_part[4],
        fc1_grad,
        fc1_part,
        fc2_grad,
        token_part[5],
    )


def solution(mesh):
    in_specs = (
        P(("dp", "row", "col"), None),
        P("row"),
        P("row"),
        P("row", None, "col"),
        P("col"),
        P("col"),
        P("col", "row"),
        P("row"),
        P("row"),
        P("row"),
        P("row", "col"),
        P("col"),
        P("col", "row"),
        P("row"),
        P(("dp", "row", "col"), None),
        P(),
        P(),
    )
    out_specs = (
        P(("dp", "row", "col"), None),
        P(),
        P(("dp", "row", "col"), None),
        P("row"),
        P("row"),
        P("row", None, "col"),
        P("col"),
        P("col"),
        P("col", "row"),
        P("row"),
        P("row"),
        P("row"),
        P("row", "col"),
        P("col"),
        P("col", "row"),
        P("row"),
    )
    return jax.shard_map(local, mesh=mesh, in_specs=in_specs, out_specs=out_specs, check_vma=False)
```

profile of v0, /device:TPU:0, one launch (start us, length us, event | category | flops | bytes accessed | tf_op | source)
XLA Modules:
  0.0 1376.4 jit_solution(3440307325007686870)
XLA Ops:
  23.3 12.9 all-gather.19.cloned.1.call-done
  36.3 13.1 all-gather.11.cloned.1.call-done
  49.4 120.7 %all-gather.9.cloned.1.call-done = bf16[3136,1024]{1,0:T(8,128)(2,1)} async-done(((bf16[784,1024]{1,0:T(8,128)(2,1)}), bf16[3136,1024]{1,0:T(8,128)(2,1)}) %all-gather.9.cloned.1.call-update) | async-done | bytes 6422544 | tf_op jit(solution)/shard_map/all_gather | solution.py:157
  170.1 9.3 add_convert_fusion
  179.4 14.6 %reshape.167 = bf16[2,1568,3,4,64]{4,3,1,0,2:T(4,128)(2,1)} reshape(bf16[3136,3,256]{2,0,1:T(8,128)(2,1)} %add_convert_fusion) | data formatting | bytes 9633792 | tf_op jit(solution)/shard_map/reshape | solution.py:170
  194.0 15.6 %copy.62 = bf16[2,1568,3,4,64]{1,4,3,2,0:T(8,128)(2,1)} copy(bf16[2,1568,3,4,64]{4,3,1,0,2:T(4,128)(2,1)} %reshape.167) | data formatting | bytes 9633792 | tf_op jit(solution)/shard_map/while | solution.py:171
  209.5 100.1 %while.22 = (s32[]{:T(128)}, bf16[2,1568,4,64]{1,3,2,0:T(8,128)(2,1)S(1)}, f32[2,4,1568]{2,1,0:T(4,128)S(1)}, bf16[2,1568,3,4,64]{1,4,3,2,0:T(8,128)(2,1)}, s32[2]{0:T(128)S(1)}, /*index=5*/s32[]{:T(128)}) while((s32[]{:T(128)}, bf16[2,1568,4,64]{1,3,2,0:T(8,128)(2,1)S(1)}, f32[2,4,1568]{2,1,0:T(4,128)S(1)}, ...), condition=%wide.region_7.8_spmd, body=%wide.region_2.7_spmd.sunk | while | flops 2588079616 | bytes 208644768 | solution.py:171
  224.7 9.1 fusion.114
  233.8 8.6 exponential_reduce_fusion.4
  242.5 8.9 fusion.117
  251.4 8.8 fusion.116
  274.1 9.0 fusion.114
  283.1 8.5 exponential_reduce_fusion.4
  291.7 8.8 fusion.117
  300.5 8.8 fusion.116
  324.3 78.0 %all_gather.40 = bf16[4096]{0:T(1024)(128)(2,1)S(1)} all-gather(bf16[1024]{0:T(1024)(128)(2,1)S(1)} %copy-done.38), channel_id=1, replica_groups=mesh['dp'=4,'row'=2,'col'=4] {'col'}, dimensions={0}, use_global_device_ids=true | all-gather | bytes 10240 | tf_op jit(solution)/shard_map/all_gather | solution.py:188
  412.1 15.9 %multiply_convert_fusion.2 = (bf16[784,4096]{1,0:T(8,128)(2,1)}, f32[784,4096]{1,0:T(8,128)}) fusion(f32[4096]{0:T(1024)S(1)} %convert_element_type.142, bf16[1024,4096]{1,0:T(8,128)(2,1)} %all-gather.17.cloned.1.call-done, f32[784,1024]{1,0:T(8,128)} %copy-done.10, f32[1024]{0:T(1024)S(1)} %bitcast.272, f32[1024]{0:T(1024)S(1)} %bitcast.262, ...), kind=kOutput, calls=%fused_computation.70 | convolution fusion | flops 6599950336 | bytes 30898304 | tf_op jit(solution)/shard_map/dot_general | solution.py:190
  428.0 121.4 %all-gather.21.cloned.1.call-done = bf16[4096,1024]{1,0:T(8,128)(2,1)} async-done(((bf16[1024,1024]{1,0:T(8,128)(2,1)}), bf16[4096,1024]{1,0:T(8,128)(2,1)}) %all-gather.21.cloned.1.call-update) | async-done | bytes 8388624 | tf_op jit(solution)/shard_map/all_gather | solution.py:187
  549.3 12.4 convert_reduce_fusion.3
  561.7 17.8 %convert_reduce_fusion = (f32[4096]{0:T(1024)}, bf16[784,4096]{1,0:T(8,128)(2,1)}) fusion(f32[784,4096]{1,0:T(8,128)} %get-tuple-element.202, f32[4096]{0:T(1024)S(1)} %convert_element_type.142, bf16[784,1024]{1,0:T(8,128)(2,1)S(1)} %get-tuple-element.162, bf16[4096,1024]{1,0:T(8,128)(2,1)} %all-gather.21.cloned.1.call-done), kind=kOutput, calls=%fused_computation.69 | convolution fusion | flops 6618411008 | bytes 29294592 | tf_op jit(solution)/shard_map/dot_general | solution.py:200
  579.5 11.1 multiply_reduce_fusion.2
  598.9 15.1 %convolution_convert_fusion = bf16[1024,4096]{1,0:T(8,128)(2,1)} fusion(bf16[784,4096]{1,0:T(8,128)(2,1)} %get-tuple-element.207, f32[784,1024]{1,0:T(8,128)} %copy-done.10, f32[1024]{0:T(1024)S(1)} %bitcast.273, f32[1024]{0:T(1024)S(1)} %bitcast.265, f32[784]{0:T(1024)S(1)} %add_rsqrt_fusion, f32[784]{0:T(1024)S(1)} %broadcast_multiply_fusion.5), kind=kOutput, calls=%fused_computation.74 | convolution fusion | flops 6584877056 | bytes 18036864 | tf_op jit(solution)/shard_map/dot_general | solution.py:203
  622.4 14.2 %convolution_convert_fusion.1 = bf16[4096,1024]{1,0:T(8,128)(2,1)} fusion(bf16[784,4096]{1,0:T(8,128)(2,1)} %get-tuple-element.201, bf16[784,1024]{1,0:T(8,128)(2,1)S(1)} %copy-done.52), kind=kOutput, calls=%fused_computation.75 | convolution fusion | flops 6580862976 | bytes 16416768 | tf_op jit(solution)/shard_map/dot_general | solution.py:202
  636.7 61.9 %all-to-all-done.1 = bf16[784,4,256]{2,0,1:T(8,128)(2,1)S(1)} async-done(((bf16[784,4,256]{2,0,1:T(8,128)(2,1)}), bf16[784,4,256]{2,0,1:T(8,128)(2,1)S(1)}, u32[]{:S(2)}, u32[]{:S(2)}) %all-to-all-start.1) | async-done | bytes 1605664 | tf_op jit(solution)/shard_map/all_to_all | solution.py:226
  708.9 258.5 %while.23 = (s32[]{:T(128)}, bf16[2,1568,3,4,64]{1,4,3,2,0:T(8,128)(2,1)}, bf16[2,1568,3,4,64]{1,4,3,2,0:T(8,128)(2,1)}, s32[2]{0:T(128)S(1)}, f32[2,4,1568]{2,1...) while((s32[]{:T(128)}, bf16[2,1568,3,4,64]{1,4,3,2,0:T(8,128)(2,1)}, ...), condition=%wide.region_18.19_spmd, body=%wide.region_15.18_spmd.sunk | while | flops 6394224128 | bytes 484584864 | solution.py:229
  726.9 11.6 fusion.126
  740.5 14.7 %multiply_reduce_fusion.9 = (f32[4,784]{1,0:T(4,128)S(1)}, f32[4,784,1568]{2,1,0:T(8,128)}) fusion(f32[4,784,1568]{2,1,0:T(8,128)} %fusion.126, f32[4,784]{1,0:T(4,128)S(1)} %get-tuple-element.296, bf16[1568,3,4,64]{0,3,2,1:T(8,128)(2,1)S(1)} %dynamic-slice_bitcast_fusion.21, pred[1568]{0:T(1024)(128)(4,1)S(1)} %iota_compare_fusion.6), kind=kOutput, calls=%fused_computation.25.clone.1 | convolution fusion | flops 653990848 | bytes 40677632 | tf_op jit(solution)/shard_map/while/body/eval_jaxpr/ihd,jhd->hij/dot_general | solution.py:40
  755.2 13.8 %multiply_convert_fusion.8 = bf16[4,784,1568]{2,1,0:T(8,128)(2,1)S(1)} fusion(f32[4,784,1568]{2,1,0:T(8,128)} %get-tuple-element.297, f32[4,784,1568]{2,1,0:T(8,128)} %fusion.126, f32[4,784]{1,0:T(4,128)S(1)} %get-tuple-element.301), kind=kLoop, calls=%fused_computation.24.clone.1 | loop fusion | flops 14751744 | bytes 49185024 | tf_op jit(solution)/shard_map/while/body/eval_jaxpr/convert_element_type | solution.py:87
  773.0 10.9 fusion.129
  783.9 14.1 %multiply_reduce_fusion.10 = (f32[4,784]{1,0:T(4,128)S(1)}, f32[4,784,1568]{2,1,0:T(8,128)}) fusion(f32[4,784,1568]{2,1,0:T(8,128)} %fusion.129, f32[4,784]{1,0:T(4,128)S(1)} %get-tuple-element.298, bf16[1568,3,4,64]{0,3,2,1:T(8,128)(2,1)S(1)} %dynamic-slice_bitcast_fusion.21, pred[1568]{0:T(1024)(128)(4,1)S(1)} %iota_compare_fusion.6), kind=kOutput, calls=%fused_computation.28.clone.1 | convolution fusion | flops 653990848 | bytes 40677632 | tf_op jit(solution)/shard_map/while/body/eval_jaxpr/ihd,jhd->hij/dot_general | solution.py:40
  798.0 13.9 %multiply_convert_fusion.7 = bf16[4,784,1568]{2,1,0:T(8,128)(2,1)S(1)} fusion(f32[4,784,1568]{2,1,0:T(8,128)} %get-tuple-element.299, f32[4,784,1568]{2,1,0:T(8,128)} %fusion.129, f32[4,784]{1,0:T(4,128)S(1)} %get-tuple-element.300), kind=kLoop, calls=%fused_computation.27.clone.1 | loop fusion | flops 14751744 | bytes 49185024 | tf_op jit(solution)/shard_map/while/body/eval_jaxpr/convert_element_type | solution.py:87
  835.3 9.1 fusion.130
  848.1 11.4 fusion.126
  861.6 14.5 %multiply_reduce_fusion.9 = (f32[4,784]{1,0:T(4,128)S(1)}, f32[4,784,1568]{2,1,0:T(8,128)}) fusion(f32[4,784,1568]{2,1,0:T(8,128)} %fusion.126, f32[4,784]{1,0:T(4,128)S(1)} %get-tuple-element.296, bf16[1568,3,4,64]{0,3,2,1:T(8,128)(2,1)S(1)} %dynamic-slice_bitcast_fusion.21, pred[1568]{0:T(1024)(128)(4,1)S(1)} %iota_compare_fusion.6), kind=kOutput, calls=%fused_computation.25.clone.1 | convolution fusion | flops 653990848 | bytes 40677632 | tf_op jit(solution)/shard_map/while/body/eval_jaxpr/ihd,jhd->hij/dot_general | solution.py:40
  876.1 14.5 %multiply_convert_fusion.8 = bf16[4,784,1568]{2,1,0:T(8,128)(2,1)S(1)} fusion(f32[4,784,1568]{2,1,0:T(8,128)} %get-tuple-element.297, f32[4,784,1568]{2,1,0:T(8,128)} %fusion.126, f32[4,784]{1,0:T(4,128)S(1)} %get-tuple-element.301), kind=kLoop, calls=%fused_computation.24.clone.1 | loop fusion | flops 14751744 | bytes 49185024 | tf_op jit(solution)/shard_map/while/body/eval_jaxpr/convert_element_type | solution.py:87
  894.5 11.0 fusion.129
  905.5 13.9 %multiply_reduce_fusion.10 = (f32[4,784]{1,0:T(4,128)S(1)}, f32[4,784,1568]{2,1,0:T(8,128)}) fusion(f32[4,784,1568]{2,1,0:T(8,128)} %fusion.129, f32[4,784]{1,0:T(4,128)S(1)} %get-tuple-element.298, bf16[1568,3,4,64]{0,3,2,1:T(8,128)(2,1)S(1)} %dynamic-slice_bitcast_fusion.21, pred[1568]{0:T(1024)(128)(4,1)S(1)} %iota_compare_fusion.6), kind=kOutput, calls=%fused_computation.28.clone.1 | convolution fusion | flops 653990848 | bytes 40677632 | tf_op jit(solution)/shard_map/while/body/eval_jaxpr/ihd,jhd->hij/dot_general | solution.py:40
  919.5 13.9 %multiply_convert_fusion.7 = bf16[4,784,1568]{2,1,0:T(8,128)(2,1)S(1)} fusion(f32[4,784,1568]{2,1,0:T(8,128)} %get-tuple-element.299, f32[4,784,1568]{2,1,0:T(8,128)} %fusion.129, f32[4,784]{1,0:T(4,128)S(1)} %get-tuple-element.300), kind=kLoop, calls=%fused_computation.27.clone.1 | loop fusion | flops 14751744 | bytes 49185024 | tf_op jit(solution)/shard_map/while/body/eval_jaxpr/convert_element_type | solution.py:87
  956.4 9.0 fusion.130
  967.4 10.0 copy.70
  977.4 10.9 convert_element_type.156
  988.4 10.0 fusion.55
  1000.4 16.0 %copy.80 = bf16[2,1568,3,4,64]{4,3,2,1,0:T(4,128)(2,1)} copy(bf16[2,1568,3,4,64]{1,4,3,2,0:T(8,128)(2,1)} %get-tuple-element.78) | data formatting | bytes 9633792 | tf_op jit(solution)/shard_map/convert_element_type | solution.py:235
  1016.4 20.6 %reshape.166 = bf16[3136,3,256]{2,1,0:T(4,128)(2,1)} reshape(bf16[2,1568,3,4,64]{4,3,2,1,0:T(4,128)(2,1)} %copy.80) | data formatting | bytes 9633792 | tf_op jit(solution)/shard_map/convert_element_type | solution.py:235
  1046.6 234.9 %all-to-all-done.2 = bf16[3136,3,256]{2,1,0:T(4,128)(2,1)} async-done(((bf16[3136,3,256]{2,1,0:T(4,128)(2,1)}), bf16[3136,3,256]{2,1,0:T(4,128)(2,1)}, u32[]{:S(2)}, u32[]{:S(2)}) %all-to-all-start.2) | async-done | bytes 4816928 | tf_op jit(solution)/shard_map/all_to_all | solution.py:240
  1289.7 9.6 reshape.159
  1299.4 10.5 fusion.52
  1310.0 39.1 %all-reduce = (f32[]{:T(128)}, f32[6,1024]{1,0:T(8,128)S(1)}, f32[2,1024]{1,0:T(2,128)S(1)}, f32[4096]{0:T(1024)S(1)}) all-reduce(f32[]{:T(128)} %get-tuple-element.181, f32[6,1024]{1,0:T(8,128)S(1)} %stack.90, f32[2,1024]{1,0:T(2,128)S(1)} %maximum_dynamic-update-slice_fusion, ...), channel_id=1, replica_groups=mesh['dp'=4,'row'=2,'col'=4] {'dp','row','col'}, use_global_device_ids=true, to_apply=%region_11.12 | all-reduce | flops 12289 | bytes 98312 | tf_op jit(solution)/shard_map/psum | solution.py:273
  (295 shorter events, 199.4 us)
Async XLA Ops:
  7.3 15.7 %all-gather.15.cloned.1.call-start = ((), (), s32[]{:S(2)}) async-start(), calls=%async_computation.13 | async-start | bytes 3145728 | tf_op jit(solution)/shard_map/all_gather | solution.py:135
  8.0 28.3 %all-gather.19.cloned.1.call-start = ((), (), s32[]{:S(2)}) async-start(), calls=%async_computation.15 | async-start | bytes 3145728 | tf_op jit(solution)/shard_map/all_gather | solution.py:136
  8.7 40.7 %all-gather.11.cloned.1.call-start = ((), (), s32[]{:S(2)}) async-start(), calls=%async_computation.11 | async-start | bytes 2359296 | tf_op jit(solution)/shard_map/all_gather | solution.py:133
  11.1 159.0 %all-gather.9.cloned.1.call-start = ((), (), s32[]{:S(2)}) async-start(), calls=%async_computation.10 | async-start | bytes 8028160 | tf_op jit(solution)/shard_map/all_gather | solution.py:157
  17.2 388.1 %all-gather.13.cloned.1.call-start = ((), (), s32[]{:S(2)}) async-start(), calls=%async_computation.12 | async-start | bytes 2621440 | tf_op jit(solution)/shard_map/all_gather | solution.py:176
  19.6 392.4 %all-gather.17.cloned.1.call-start = ((), (), s32[]{:S(2)}) async-start(), calls=%async_computation.14 | async-start | bytes 10485760 | tf_op jit(solution)/shard_map/all_gather | solution.py:186
  23.0 526.3 %all-gather.21.cloned.1.call-start = ((), (), s32[]{:S(2)}) async-start(), calls=%async_computation.16 | async-start | bytes 10485760 | tf_op jit(solution)/shard_map/all_gather | solution.py:187
  317.5 84.8 %copy-start.46 = (s32[16]{0:T(128)S(1)}, s32[16]{0:T(128)}, u32[]{:S(2)}) copy-start(s32[16]{0:T(128)} %param.37) | copy-start | bytes 196
  317.5 85.0 %copy-start.22 = (s32[25088]{0:T(1024)S(1)}, s32[25088]{0:T(1024)}, u32[]{:S(2)}) copy-start(s32[25088]{0:T(1024)} %param.36) | copy-start | bytes 301060
  320.5 84.8 %copy-start.7 = (bf16[784,1024]{1,0:T(8,128)(2,1)S(1)}, bf16[784,1024]{1,0:T(8,128)(2,1)}, u32[]{:S(2)}) copy-start(bf16[784,1024]{1,0:T(8,128)(2,1)} %param.21) | copy-start | bytes 4816900
  320.5 84.8 %copy-start.37 = (f32[1,1024]{1,0:T(1,128)S(1)}, f32[1,1024]{1,0:T(1,128)}, u32[]{:S(2)}) copy-start(f32[1,1024]{1,0:T(1,128)} %get-tuple-element.192) | copy-start | bytes 12292
  320.5 83.4 %all-to-all-start = ((bf16[4,784,256]{2,1,0:T(8,128)(2,1)}), bf16[4,784,256]{2,1,0:T(8,128)(2,1)S(1)}, u32[]{:S(2)}, u32[]{:S(2)}) async-start(bf16[4,784,256]{2,1,0:T(8,128)(2,1)} %reshape.164), calls=%async_computation | async-start | bytes 3211264 | tf_op jit(solution)/shard_map/all_to_all | solution.py:179
  324.2 664.1 %reduce-scatter.10.cloned.1.call-start = ((), (), s32[]{:S(2)}) async-start(), calls=%async_computation.19 | async-start | bytes 2621440 | tf_op jit(solution)/shard_map/reduce_scatter | solution.py:220
  412.1 137.2 %copy-start.11 = (f32[784,1024]{1,0:T(8,128)S(1)}, f32[784,1024]{1,0:T(8,128)}, u32[]{:S(2)}) copy-start(f32[784,1024]{1,0:T(8,128)} %copy-done.10) | copy-start | bytes 9633796
  412.1 137.2 %copy-start.36 = (f32[1,1024]{1,0:T(1,128)S(1)}, f32[1,1024]{1,0:T(1,128)}, u32[]{:S(2)}) copy-start(f32[1,1024]{1,0:T(1,128)} %get-tuple-element.191) | copy-start | bytes 12292
  549.3 30.2 %slice-start.5 = ((s8[8388608]{0:T(1024)(128)(4,1)}), s8[4194304]{0:T(1024)(128)(4,1)S(1)}, s32[]{:S(2)}) async-start(s8[8388608]{0:T(1024)(128)(4,1)} %bitcast.286), calls=%async_computation.31 | async-start | bytes 8388608
  561.7 17.8 %copy-start.51 = (bf16[784,1024]{1,0:T(8,128)(2,1)}, bf16[784,1024]{1,0:T(8,128)(2,1)S(1)}, u32[]{:S(2)}) copy-start(bf16[784,1024]{1,0:T(8,128)(2,1)S(1)} %get-tuple-element.162) | copy-start | bytes 4816900
  561.7 17.8 %slice-start.6 = ((s8[8388608]{0:T(1024)(128)(4,1)}), s8[4194304]{0:T(1024)(128)(4,1)S(1)}, s32[]{:S(2)}) async-start(s8[8388608]{0:T(1024)(128)(4,1)} %bitcast.286), calls=%async_computation.32 | async-start | bytes 8388608
  579.5 11.1 copy-start.12
  579.5 11.1 copy-start.15
  595.1 18.9 %copy-start.9 = (f32[784,1024]{1,0:T(8,128)}, f32[784,1024]{1,0:T(8,128)S(1)}, u32[]{:S(2)}) copy-start(f32[784,1024]{1,0:T(8,128)S(1)} %get-tuple-element.164) | copy-start | bytes 9633796
  598.9 399.6 %reduce-scatter.14.cloned.1.call-start = ((), (), s32[]{:S(2)}) async-start(), calls=%async_computation.21 | async-start | bytes 10485760 | tf_op jit(solution)/shard_map/reduce_scatter | solution.py:205
  618.8 79.8 %all-to-all-start.1 = ((bf16[784,4,256]{2,0,1:T(8,128)(2,1)}), bf16[784,4,256]{2,0,1:T(8,128)(2,1)S(1)}, u32[]{:S(2)}, u32[]{:S(2)}) async-start(bf16[784,4,256]{2,0,1:T(8,128)(2,1)} %bitcast.170), calls=%async_computation.1 | async-start | bytes 3211264 | tf_op jit(solution)/shard_map/all_to_all | solution.py:226
  622.3 376.9 %reduce-scatter.18.cloned.1.call-start = ((), (), s32[]{:S(2)}) async-start(), calls=%async_computation.23 | async-start | bytes 10485760 | tf_op jit(solution)/shard_map/reduce_scatter | solution.py:208
  636.6 409.9 %reduce-scatter.12.cloned.1.call-start = ((), (), s32[]{:S(2)}) async-start(), calls=%async_computation.20 | async-start | bytes 786432 | tf_op jit(solution)/shard_map/reduce_scatter | solution.py:280
  726.8 57.0 %copy-start.3 = (bf16[1568,3,4,64]{0,3,2,1:T(8,128)(2,1)}, bf16[1568,3,4,64]{0,3,2,1:T(8,128)(2,1)S(1)}, u32[]{:S(2)}) copy-start(bf16[1568,3,4,64]{0,3,2,1:T(8,128)(2,1)S(1)} %dynamic-slice_bitcast_fusion.21) | copy-start | bytes 7225348 | tf_op jit(solution)/shard_map/while
  811.9 20.3 %slice-start = ((s8[20873216]{0:T(1024)(128)(4,1)}), s8[4194304]{0:T(1024)(128)(4,1)S(1)}, s32[]{:S(2)}) async-start(s8[20873216]{0:T(1024)(128)(4,1)} %bitcast.249), calls=%async_computation.26 | async-start | bytes 8388608 | tf_op jit(solution)/shard_map/while
  811.9 20.2 %slice-start.1 = ((s8[20873216]{0:T(1024)(128)(4,1)}), s8[4096000]{0:T(1024)(128)(4,1)S(1)}, s32[]{:S(2)}) async-start(s8[20873216]{0:T(1024)(128)(4,1)} %bitcast.249), calls=%async_computation.27 | async-start | bytes 8192000 | tf_op jit(solution)/shard_map/while
  818.4 13.8 %slice-start.2 = ((s8[20873216]{0:T(1024)(128)(4,1)}), s8[4194304]{0:T(1024)(128)(4,1)S(1)}, s32[]{:S(2)}) async-start(s8[20873216]{0:T(1024)(128)(4,1)} %bitcast.249), calls=%async_computation.28 | async-start | bytes 8388608 | tf_op jit(solution)/shard_map/while
  818.4 13.8 %slice-start.3 = ((s8[20873216]{0:T(1024)(128)(4,1)}), s8[4194304]{0:T(1024)(128)(4,1)S(1)}, s32[]{:S(2)}) async-start(s8[20873216]{0:T(1024)(128)(4,1)} %bitcast.249), calls=%async_computation.29 | async-start | bytes 8388608 | tf_op jit(solution)/shard_map/while
  848.1 57.4 %copy-start.3 = (bf16[1568,3,4,64]{0,3,2,1:T(8,128)(2,1)}, bf16[1568,3,4,64]{0,3,2,1:T(8,128)(2,1)S(1)}, u32[]{:S(2)}) copy-start(bf16[1568,3,4,64]{0,3,2,1:T(8,128)(2,1)S(1)} %dynamic-slice_bitcast_fusion.21) | copy-start | bytes 7225348 | tf_op jit(solution)/shard_map/while
  933.4 19.8 %slice-start = ((s8[20873216]{0:T(1024)(128)(4,1)}), s8[4194304]{0:T(1024)(128)(4,1)S(1)}, s32[]{:S(2)}) async-start(s8[20873216]{0:T(1024)(128)(4,1)} %bitcast.249), calls=%async_computation.26 | async-start | bytes 8388608 | tf_op jit(solution)/shard_map/while
  933.4 19.8 %slice-start.1 = ((s8[20873216]{0:T(1024)(128)(4,1)}), s8[4096000]{0:T(1024)(128)(4,1)S(1)}, s32[]{:S(2)}) async-start(s8[20873216]{0:T(1024)(128)(4,1)} %bitcast.249), calls=%async_computation.27 | async-start | bytes 8192000 | tf_op jit(solution)/shard_map/while
  939.8 13.4 slice-start.2
  939.8 13.4 slice-start.3
  988.4 58.2 %reduce-scatter.8.cloned.1.call-start = ((), (), s32[]{:S(2)}) async-start(), calls=%async_computation.18 | async-start | bytes 2359296 | tf_op jit(solution)/shard_map/reduce_scatter | solution.py:277
  998.4 48.1 %reduce-scatter.16.cloned.1.call-start = ((), (), s32[]{:S(2)}) async-start(), calls=%async_computation.22 | async-start | bytes 3145728 | tf_op jit(solution)/shard_map/reduce_scatter | solution.py:283
  999.2 47.4 %reduce-scatter.20.cloned.1.call-start = ((), (), s32[]{:S(2)}) async-start(), calls=%async_computation.24 | async-start | bytes 3145728 | tf_op jit(solution)/shard_map/reduce_scatter | solution.py:286
  999.8 299.5 %all-gather.23.cloned.1.call-start = ((), (), s32[]{:S(2)}) async-start(), calls=%async_computation.17 | async-start | bytes 7864320 | tf_op jit(solution)/shard_map/all_gather | solution.py:177
  1037.0 244.6 %all-to-all-start.2 = ((bf16[3136,3,256]{2,1,0:T(4,128)(2,1)}), bf16[3136,3,256]{2,1,0:T(4,128)(2,1)}, u32[]{:S(2)}, u32[]{:S(2)}) async-start(bf16[3136,3,256]{2,1,0:T(4,128)(2,1)} %reshape.166), calls=%async_computation.2 | async-start | bytes 12845056 | tf_op jit(solution)/shard_map/all_to_all | solution.py:240
  1042.3 319.6 %all-reduce.4.cloned.1.call-start = ((), (), s32[]{:S(2)}) async-start(), calls=%async_computation.25 | async-start | bytes 6291456 | tf_op jit(solution)/shard_map/psum | solution.py:291
  1289.7 9.6 copy-start.26
  1289.7 9.6 copy-start.28
  1299.3 10.6 copy-start.29
  1299.3 10.6 copy-start.32
  1299.4 10.6 copy-start.33
  1299.4 10.6 copy-start.34
  1299.4 10.6 copy-start.31
  (42 other events, 197.7 us)
Sparse Core Ops, SparseCore 0:
  9.6 13.2 all-gather.14
  24.5 11.7 all-gather.18
  38.4 10.9 all-gather.10
  51.4 118.6 all-gather.8
  171.5 44.1 all-gather.12
  217.1 182.7 all-gather.16
  401.5 147.7 all-gather.20
  599.0 55.7 reduce-scatter.9
  657.3 151.0 reduce-scatter.13
  810.7 145.4 reduce-scatter.17
  988.5 6.2 reduce-scatter.11
  998.6 9.0 reduce-scatter.7
  1010.0 10.8 reduce-scatter.15
  1023.0 10.7 reduce-scatter.19
  1035.3 229.2 all-gather.22
  1268.2 93.6 all-reduce.3
where the time goes:
time: 1380 us
  waiting for transfers between devices  577 us (42%)
  matrix products  359 us (26%)
  local copies, waits for them, and re-layouts  159 us (12%)
  blocking collectives  121 us (9%)
  other arithmetic  112 us (8%)
  loops' own time  17.3 us (1%)
  between operations  17.3 us (1%)
    all_to_all x1, waiting for transfers between devices, local(): lax.all_to_all(grads_packed.reshape(group_rows, 3, head_width), 'col', sp...  235 us
    all_gather x1, waiting for transfers between devices, local(): lax.all_gather(fc2_full, 'col', axis=0, tiled=True)  121 us
    all_gather x1, waiting for transfers between devices, local(): tokens_one = lax.all_gather(norm_one, 'col', axis=0, tiled=True)  121 us
    dot_general x8, matrix products, masked_scores(): jnp.einsum('ihd,jhd->hij', queries, key_rows, preferred_element_type=jnp....  82.4 us
    all_gather x1, blocking collectives, local(): lax.all_gather(fc1_bias, 'col', axis=0, tiled=True)  78 us
    all_to_all x1, waiting for transfers between devices, local(): lax.all_to_all(grad_attended_rows, 'col', split_axis=1, concat_axis=0, ti...  61.9 us
    convert_element_type x4, local copies, waits for them, and re-layouts, local(): grads_packed.reshape(group_rows, 3 * head_width).astype(jnp.bfloat16)  57.5 us
    convert_element_type x4, other arithmetic, attend_clip_back(): grad_logits = (probs * (grad_probs - jnp.sum(probs * grad_probs, axis=-1,...  56.2 us
  transfers between devices with their start and end apart: 19, of which 8 were waited for; matrix products, arithmetic and copies ran while one was open for 41% of the time, Pallas kernels for 0%

commit v1 on v0

--- a/solution.py
+++ b/solution.py
@@ -271,7 +271,7 @@
         (0, col_index * head_width),
     )
     token_sums, head_sums, fc1_sums, loss_sum = lax.psum(
-        (token_vectors, head_vectors, fc1_bias_sum, numerator), ("dp", "row", "col")
+        lax.psum((token_vectors, head_vectors, fc1_bias_sum, numerator), ("row", "col")), "dp"
     )
     qkv_rows, proj_cols, fc1_rows, fc2_cols = (
         lax.psum_scatter(

time: 1380 us -> 1390 us (level)
    psum x1 -> x2, blocking collectives: 39.1 us -> 46.5 us  [the longest x1 26.9 us: local(): lax.psum((token_vectors, head_vectors, fc1_bias_sum, numerator), ('row',...]
  transfers between devices with their start and end apart: 19 -> 19, of which waited for: 8 -> 7; matrix products, arithmetic and copies ran while one was open for 41% -> 41% of each run, Pallas kernels for 0% -> 0%
where the time goes in v1:
time: 1390 us; the launch traced here: 1380 us
  waiting for transfers between devices  571 us (41%)
  matrix products  359 us (26%)
  local copies, waits for them, and re-layouts  159 us (11%)
  blocking collectives  129 us (9%)
  other arithmetic  112 us (8%)
  loops' own time  17.3 us (1%)
  between operations  17.3 us (1%)
    all_to_all x1, waiting for transfers between devices, local(): lax.all_to_all(grads_packed.reshape(group_rows, 3, head_width), 'col', sp...  235 us
    all_gather x1, waiting for transfers between devices, local(): lax.all_gather(fc2_full, 'col', axis=0, tiled=True)  121 us
    all_gather x1, waiting for transfers between devices, local(): tokens_one = lax.all_gather(norm_one, 'col', axis=0, tiled=True)  121 us
    dot_general x8, matrix products, masked_scores(): jnp.einsum('ihd,jhd->hij', queries, key_rows, preferred_element_type=jnp....  82.5 us
    all_gather x1, blocking collectives, local(): lax.all_gather(fc1_bias, 'col', axis=0, tiled=True)  78 us
    all_to_all x1, waiting for transfers between devices, local(): lax.all_to_all(grad_attended_rows, 'col', split_axis=1, concat_axis=0, ti...  61.9 us
    convert_element_type x4, local copies, waits for them, and re-layouts, local(): grads_packed.reshape(group_rows, 3 * head_width).astype(jnp.bfloat16)  57.6 us
    convert_element_type x4, other arithmetic, attend_clip_back(): grad_logits = (probs * (grad_probs - jnp.sum(probs * grad_probs, axis=-1,...  56.2 us
  transfers between devices with their start and end apart: 19, of which 7 were waited for; matrix products, arithmetic and copies ran while one was open for 41% of the time, Pallas kernels for 0%

profile of v1, /device:TPU:0, one launch (start us, length us, event | category | flops | bytes accessed | tf_op | source)
XLA Modules:
  0.0 1378.2 jit_solution(15634704702560019353)
XLA Ops:
  23.3 12.9 all-gather.19.cloned.1.call-done
  36.3 13.1 all-gather.11.cloned.1.call-done
  49.4 120.7 %all-gather.9.cloned.1.call-done = bf16[3136,1024]{1,0:T(8,128)(2,1)} async-done(((bf16[784,1024]{1,0:T(8,128)(2,1)}), bf16[3136,1024]{1,0:T(8,128)(2,1)}) %all-gather.9.cloned.1.call-update) | async-done | bytes 6422544 | tf_op jit(solution)/shard_map/all_gather | solution.py:157
  170.1 9.3 add_convert_fusion
  179.4 14.6 %reshape.167 = bf16[2,1568,3,4,64]{4,3,1,0,2:T(4,128)(2,1)} reshape(bf16[3136,3,256]{2,0,1:T(8,128)(2,1)} %add_convert_fusion) | data formatting | bytes 9633792 | tf_op jit(solution)/shard_map/reshape | solution.py:170
  194.0 15.6 %copy.62 = bf16[2,1568,3,4,64]{1,4,3,2,0:T(8,128)(2,1)} copy(bf16[2,1568,3,4,64]{4,3,1,0,2:T(4,128)(2,1)} %reshape.167) | data formatting | bytes 9633792 | tf_op jit(solution)/shard_map/while | solution.py:171
  209.6 100.1 %while.22 = (s32[]{:T(128)}, bf16[2,1568,4,64]{1,3,2,0:T(8,128)(2,1)S(1)}, f32[2,4,1568]{2,1,0:T(4,128)S(1)}, bf16[2,1568,3,4,64]{1,4,3,2,0:T(8,128)(2,1)}, s32[2]{0:T(128)S(1)}, /*index=5*/s32[]{:T(128)}) while((s32[]{:T(128)}, bf16[2,1568,4,64]{1,3,2,0:T(8,128)(2,1)S(1)}, f32[2,4,1568]{2,1,0:T(4,128)S(1)}, ...), condition=%wide.region_7.8_spmd, body=%wide.region_2.7_spmd.sunk | while | flops 2588079616 | bytes 208644768 | solution.py:171
  224.8 9.1 fusion.114
  233.9 8.6 exponential_reduce_fusion.4
  242.5 8.9 fusion.117
  251.4 8.8 fusion.116
  274.2 9.0 fusion.114
  291.8 8.8 fusion.117
  300.6 8.8 fusion.116
  324.4 78.0 %all_gather.40 = bf16[4096]{0:T(1024)(128)(2,1)S(1)} all-gather(bf16[1024]{0:T(1024)(128)(2,1)S(1)} %copy-done.38), channel_id=1, replica_groups=mesh['dp'=4,'row'=2,'col'=4] {'col'}, dimensions={0}, use_global_device_ids=true | all-gather | bytes 10240 | tf_op jit(solution)/shard_map/all_gather | solution.py:188
  412.2 15.9 %multiply_convert_fusion.2 = (bf16[784,4096]{1,0:T(8,128)(2,1)}, f32[784,4096]{1,0:T(8,128)}) fusion(f32[4096]{0:T(1024)S(1)} %convert_element_type.142, bf16[1024,4096]{1,0:T(8,128)(2,1)} %all-gather.17.cloned.1.call-done, f32[784,1024]{1,0:T(8,128)} %copy-done.10, f32[1024]{0:T(1024)S(1)} %bitcast.272, f32[1024]{0:T(1024)S(1)} %bitcast.262, ...), kind=kOutput, calls=%fused_computation.70 | convolution fusion | flops 6599950336 | bytes 30898304 | tf_op jit(solution)/shard_map/dot_general | solution.py:190
  428.0 121.3 %all-gather.21.cloned.1.call-done = bf16[4096,1024]{1,0:T(8,128)(2,1)} async-done(((bf16[1024,1024]{1,0:T(8,128)(2,1)}), bf16[4096,1024]{1,0:T(8,128)(2,1)}) %all-gather.21.cloned.1.call-update) | async-done | bytes 8388624 | tf_op jit(solution)/shard_map/all_gather | solution.py:187
  549.3 12.4 convert_reduce_fusion.3
  561.7 17.8 %convert_reduce_fusion = (f32[4096]{0:T(1024)}, bf16[784,4096]{1,0:T(8,128)(2,1)}) fusion(f32[784,4096]{1,0:T(8,128)} %get-tuple-element.206, f32[4096]{0:T(1024)S(1)} %convert_element_type.142, bf16[784,1024]{1,0:T(8,128)(2,1)S(1)} %get-tuple-element.166, bf16[4096,1024]{1,0:T(8,128)(2,1)} %all-gather.21.cloned.1.call-done), kind=kOutput, calls=%fused_computation.69 | convolution fusion | flops 6618411008 | bytes 29294592 | tf_op jit(solution)/shard_map/dot_general | solution.py:200
  579.6 11.1 multiply_reduce_fusion.2
  598.9 15.1 %convolution_convert_fusion = bf16[1024,4096]{1,0:T(8,128)(2,1)} fusion(bf16[784,4096]{1,0:T(8,128)(2,1)} %get-tuple-element.211, f32[784,1024]{1,0:T(8,128)} %copy-done.10, f32[1024]{0:T(1024)S(1)} %bitcast.273, f32[1024]{0:T(1024)S(1)} %bitcast.265, f32[784]{0:T(1024)S(1)} %add_rsqrt_fusion, f32[784]{0:T(1024)S(1)} %broadcast_multiply_fusion.5), kind=kOutput, calls=%fused_computation.74 | convolution fusion | flops 6584877056 | bytes 18036864 | tf_op jit(solution)/shard_map/dot_general | solution.py:203
  622.4 14.2 %convolution_convert_fusion.1 = bf16[4096,1024]{1,0:T(8,128)(2,1)} fusion(bf16[784,4096]{1,0:T(8,128)(2,1)} %get-tuple-element.205, bf16[784,1024]{1,0:T(8,128)(2,1)S(1)} %copy-done.52), kind=kOutput, calls=%fused_computation.75 | convolution fusion | flops 6580862976 | bytes 16416768 | tf_op jit(solution)/shard_map/dot_general | solution.py:202
  636.7 61.9 %all-to-all-done.1 = bf16[784,4,256]{2,0,1:T(8,128)(2,1)S(1)} async-done(((bf16[784,4,256]{2,0,1:T(8,128)(2,1)}), bf16[784,4,256]{2,0,1:T(8,128)(2,1)S(1)}, u32[]{:S(2)}, u32[]{:S(2)}) %all-to-all-start.1) | async-done | bytes 1605664 | tf_op jit(solution)/shard_map/all_to_all | solution.py:226
  709.0 258.5 %while.23 = (s32[]{:T(128)}, bf16[2,1568,3,4,64]{1,4,3,2,0:T(8,128)(2,1)}, bf16[2,1568,3,4,64]{1,4,3,2,0:T(8,128)(2,1)}, s32[2]{0:T(128)S(1)}, f32[2,4,1568]{2,1...) while((s32[]{:T(128)}, bf16[2,1568,3,4,64]{1,4,3,2,0:T(8,128)(2,1)}, ...), condition=%wide.region_19.20_spmd, body=%wide.region_16.19_spmd.sunk | while | flops 6394224128 | bytes 484584864 | solution.py:229
  726.9 11.6 fusion.126
  740.5 14.7 %multiply_reduce_fusion.9 = (f32[4,784]{1,0:T(4,128)S(1)}, f32[4,784,1568]{2,1,0:T(8,128)}) fusion(f32[4,784,1568]{2,1,0:T(8,128)} %fusion.126, f32[4,784]{1,0:T(4,128)S(1)} %get-tuple-element.300, bf16[1568,3,4,64]{0,3,2,1:T(8,128)(2,1)S(1)} %dynamic-slice_bitcast_fusion.21, pred[1568]{0:T(1024)(128)(4,1)S(1)} %iota_compare_fusion.6), kind=kOutput, calls=%fused_computation.25.clone.1 | convolution fusion | flops 653990848 | bytes 40677632 | tf_op jit(solution)/shard_map/while/body/eval_jaxpr/ihd,jhd->hij/dot_general | solution.py:40
  755.2 13.8 %multiply_convert_fusion.8 = bf16[4,784,1568]{2,1,0:T(8,128)(2,1)S(1)} fusion(f32[4,784,1568]{2,1,0:T(8,128)} %get-tuple-element.301, f32[4,784,1568]{2,1,0:T(8,128)} %fusion.126, f32[4,784]{1,0:T(4,128)S(1)} %get-tuple-element.305), kind=kLoop, calls=%fused_computation.24.clone.1 | loop fusion | flops 14751744 | bytes 49185024 | tf_op jit(solution)/shard_map/while/body/eval_jaxpr/convert_element_type | solution.py:87
  773.0 10.9 fusion.129
  783.9 14.1 %multiply_reduce_fusion.10 = (f32[4,784]{1,0:T(4,128)S(1)}, f32[4,784,1568]{2,1,0:T(8,128)}) fusion(f32[4,784,1568]{2,1,0:T(8,128)} %fusion.129, f32[4,784]{1,0:T(4,128)S(1)} %get-tuple-element.302, bf16[1568,3,4,64]{0,3,2,1:T(8,128)(2,1)S(1)} %dynamic-slice_bitcast_fusion.21, pred[1568]{0:T(1024)(128)(4,1)S(1)} %iota_compare_fusion.6), kind=kOutput, calls=%fused_computation.28.clone.1 | convolution fusion | flops 653990848 | bytes 40677632 | tf_op jit(solution)/shard_map/while/body/eval_jaxpr/ihd,jhd->hij/dot_general | solution.py:40
  798.0 13.9 %multiply_convert_fusion.7 = bf16[4,784,1568]{2,1,0:T(8,128)(2,1)S(1)} fusion(f32[4,784,1568]{2,1,0:T(8,128)} %get-tuple-element.303, f32[4,784,1568]{2,1,0:T(8,128)} %fusion.129, f32[4,784]{1,0:T(4,128)S(1)} %get-tuple-element.304), kind=kLoop, calls=%fused_computation.27.clone.1 | loop fusion | flops 14751744 | bytes 49185024 | tf_op jit(solution)/shard_map/while/body/eval_jaxpr/convert_element_type | solution.py:87
  835.4 9.1 fusion.130
  848.1 11.4 fusion.126
  861.6 14.6 %multiply_reduce_fusion.9 = (f32[4,784]{1,0:T(4,128)S(1)}, f32[4,784,1568]{2,1,0:T(8,128)}) fusion(f32[4,784,1568]{2,1,0:T(8,128)} %fusion.126, f32[4,784]{1,0:T(4,128)S(1)} %get-tuple-element.300, bf16[1568,3,4,64]{0,3,2,1:T(8,128)(2,1)S(1)} %dynamic-slice_bitcast_fusion.21, pred[1568]{0:T(1024)(128)(4,1)S(1)} %iota_compare_fusion.6), kind=kOutput, calls=%fused_computation.25.clone.1 | convolution fusion | flops 653990848 | bytes 40677632 | tf_op jit(solution)/shard_map/while/body/eval_jaxpr/ihd,jhd->hij/dot_general | solution.py:40
  876.1 14.5 %multiply_convert_fusion.8 = bf16[4,784,1568]{2,1,0:T(8,128)(2,1)S(1)} fusion(f32[4,784,1568]{2,1,0:T(8,128)} %get-tuple-element.301, f32[4,784,1568]{2,1,0:T(8,128)} %fusion.126, f32[4,784]{1,0:T(4,128)S(1)} %get-tuple-element.305), kind=kLoop, calls=%fused_computation.24.clone.1 | loop fusion | flops 14751744 | bytes 49185024 | tf_op jit(solution)/shard_map/while/body/eval_jaxpr/convert_element_type | solution.py:87
  894.6 11.0 fusion.129
  905.6 14.0 %multiply_reduce_fusion.10 = (f32[4,784]{1,0:T(4,128)S(1)}, f32[4,784,1568]{2,1,0:T(8,128)}) fusion(f32[4,784,1568]{2,1,0:T(8,128)} %fusion.129, f32[4,784]{1,0:T(4,128)S(1)} %get-tuple-element.302, bf16[1568,3,4,64]{0,3,2,1:T(8,128)(2,1)S(1)} %dynamic-slice_bitcast_fusion.21, pred[1568]{0:T(1024)(128)(4,1)S(1)} %iota_compare_fusion.6), kind=kOutput, calls=%fused_computation.28.clone.1 | convolution fusion | flops 653990848 | bytes 40677632 | tf_op jit(solution)/shard_map/while/body/eval_jaxpr/ihd,jhd->hij/dot_general | solution.py:40
  919.5 13.9 %multiply_convert_fusion.7 = bf16[4,784,1568]{2,1,0:T(8,128)(2,1)S(1)} fusion(f32[4,784,1568]{2,1,0:T(8,128)} %get-tuple-element.303, f32[4,784,1568]{2,1,0:T(8,128)} %fusion.129, f32[4,784]{1,0:T(4,128)S(1)} %get-tuple-element.304), kind=kLoop, calls=%fused_computation.27.clone.1 | loop fusion | flops 14751744 | bytes 49185024 | tf_op jit(solution)/shard_map/while/body/eval_jaxpr/convert_element_type | solution.py:87
  956.4 9.0 fusion.130
  967.5 10.0 copy.70
  977.5 10.9 convert_element_type.156
  988.5 10.0 fusion.55
  1000.4 16.1 %copy.80 = bf16[2,1568,3,4,64]{4,3,2,1,0:T(4,128)(2,1)} copy(bf16[2,1568,3,4,64]{1,4,3,2,0:T(8,128)(2,1)} %get-tuple-element.78) | data formatting | bytes 9633792 | tf_op jit(solution)/shard_map/convert_element_type | solution.py:235
  1016.5 20.6 %reshape.166 = bf16[3136,3,256]{2,1,0:T(4,128)(2,1)} reshape(bf16[2,1568,3,4,64]{4,3,2,1,0:T(4,128)(2,1)} %copy.80) | data formatting | bytes 9633792 | tf_op jit(solution)/shard_map/convert_element_type | solution.py:235
  1046.7 234.9 %all-to-all-done.2 = bf16[3136,3,256]{2,1,0:T(4,128)(2,1)} async-done(((bf16[3136,3,256]{2,1,0:T(4,128)(2,1)}), bf16[3136,3,256]{2,1,0:T(4,128)(2,1)}, u32[]{:S(2)}, u32[]{:S(2)}) %all-to-all-start.2) | async-done | bytes 4816928 | tf_op jit(solution)/shard_map/all_to_all | solution.py:240
  1289.8 9.6 reshape.159
  1299.5 10.5 fusion.52
  1310.1 26.9 %all-reduce = (f32[]{:T(128)}, f32[6,1024]{1,0:T(8,128)S(1)}, f32[2,1024]{1,0:T(2,128)S(1)}, f32[4096]{0:T(1024)S(1)}) all-reduce(f32[]{:T(128)} %get-tuple-element.185, f32[6,1024]{1,0:T(8,128)S(1)} %stack.90, f32[2,1024]{1,0:T(2,128)S(1)} %maximum_dynamic-update-slice_fusion, ...), channel_id=1, replica_groups=mesh['dp'=4,'row'=2,'col'=4] {'row','col'}, use_global_device_ids=true, to_apply=%region_11.12 | all-reduce | flops 12289 | bytes 98312 | tf_op jit(solution)/shard_map/psum | solution.py:274
  1337.0 19.6 %all-reduce.1 = (f32[]{:T(128)}, f32[6,1024]{1,0:T(8,128)S(1)}, f32[2,1024]{1,0:T(2,128)S(1)}, f32[4096]{0:T(1024)S(1)}) all-reduce(f32[]{:T(128)} %get-tuple-element.153, f32[6,1024]{1,0:T(8,128)S(1)} %get-tuple-element.154, f32[2,1024]{1,0:T(2,128)S(1)} %get-tuple-element.155, ...), channel_id=1, replica_groups=mesh['dp'=4,'row'=2,'col'=4] {'dp'}, use_global_device_ids=true, to_apply=%region_12.13 | all-reduce | flops 12289 | bytes 98312 | tf_op jit(solution)/shard_map/psum | solution.py:273
  (296 shorter events, 202.1 us)
Async XLA Ops:
  7.3 15.7 %all-gather.15.cloned.1.call-start = ((), (), s32[]{:S(2)}) async-start(), calls=%async_computation.13 | async-start | bytes 3145728 | tf_op jit(solution)/shard_map/all_gather | solution.py:135
  8.0 28.3 %all-gather.19.cloned.1.call-start = ((), (), s32[]{:S(2)}) async-start(), calls=%async_computation.15 | async-start | bytes 3145728 | tf_op jit(solution)/shard_map/all_gather | solution.py:136
  8.7 40.7 %all-gather.11.cloned.1.call-start = ((), (), s32[]{:S(2)}) async-start(), calls=%async_computation.11 | async-start | bytes 2359296 | tf_op jit(solution)/shard_map/all_gather | solution.py:133
  11.1 159.0 %all-gather.9.cloned.1.call-start = ((), (), s32[]{:S(2)}) async-start(), calls=%async_computation.10 | async-start | bytes 8028160 | tf_op jit(solution)/shard_map/all_gather | solution.py:157
  17.2 388.2 %all-gather.13.cloned.1.call-start = ((), (), s32[]{:S(2)}) async-start(), calls=%async_computation.12 | async-start | bytes 2621440 | tf_op jit(solution)/shard_map/all_gather | solution.py:176
  19.6 392.5 %all-gather.17.cloned.1.call-start = ((), (), s32[]{:S(2)}) async-start(), calls=%async_computation.14 | async-start | bytes 10485760 | tf_op jit(solution)/shard_map/all_gather | solution.py:186
  23.0 526.3 %all-gather.21.cloned.1.call-start = ((), (), s32[]{:S(2)}) async-start(), calls=%async_computation.16 | async-start | bytes 10485760 | tf_op jit(solution)/shard_map/all_gather | solution.py:187
  317.6 84.9 %copy-start.46 = (s32[16]{0:T(128)S(1)}, s32[16]{0:T(128)}, u32[]{:S(2)}) copy-start(s32[16]{0:T(128)} %param.37) | copy-start | bytes 196
  317.6 85.1 %copy-start.22 = (s32[25088]{0:T(1024)S(1)}, s32[25088]{0:T(1024)}, u32[]{:S(2)}) copy-start(s32[25088]{0:T(1024)} %param.36) | copy-start | bytes 301060
  320.6 84.8 %copy-start.7 = (bf16[784,1024]{1,0:T(8,128)(2,1)S(1)}, bf16[784,1024]{1,0:T(8,128)(2,1)}, u32[]{:S(2)}) copy-start(bf16[784,1024]{1,0:T(8,128)(2,1)} %param.21) | copy-start | bytes 4816900
  320.6 84.8 %copy-start.37 = (f32[1,1024]{1,0:T(1,128)S(1)}, f32[1,1024]{1,0:T(1,128)}, u32[]{:S(2)}) copy-start(f32[1,1024]{1,0:T(1,128)} %get-tuple-element.196) | copy-start | bytes 12292
  320.6 83.4 %all-to-all-start = ((bf16[4,784,256]{2,1,0:T(8,128)(2,1)}), bf16[4,784,256]{2,1,0:T(8,128)(2,1)S(1)}, u32[]{:S(2)}, u32[]{:S(2)}) async-start(bf16[4,784,256]{2,1,0:T(8,128)(2,1)} %reshape.164), calls=%async_computation | async-start | bytes 3211264 | tf_op jit(solution)/shard_map/all_to_all | solution.py:179
  324.3 664.1 %reduce-scatter.10.cloned.1.call-start = ((), (), s32[]{:S(2)}) async-start(), calls=%async_computation.19 | async-start | bytes 2621440 | tf_op jit(solution)/shard_map/reduce_scatter | solution.py:220
  412.1 137.2 %copy-start.11 = (f32[784,1024]{1,0:T(8,128)S(1)}, f32[784,1024]{1,0:T(8,128)}, u32[]{:S(2)}) copy-start(f32[784,1024]{1,0:T(8,128)} %copy-done.10) | copy-start | bytes 9633796
  412.2 137.2 %copy-start.36 = (f32[1,1024]{1,0:T(1,128)S(1)}, f32[1,1024]{1,0:T(1,128)}, u32[]{:S(2)}) copy-start(f32[1,1024]{1,0:T(1,128)} %get-tuple-element.195) | copy-start | bytes 12292
  549.3 30.2 %slice-start.5 = ((s8[8388608]{0:T(1024)(128)(4,1)}), s8[4194304]{0:T(1024)(128)(4,1)S(1)}, s32[]{:S(2)}) async-start(s8[8388608]{0:T(1024)(128)(4,1)} %bitcast.286), calls=%async_computation.31 | async-start | bytes 8388608
  561.7 17.8 %copy-start.51 = (bf16[784,1024]{1,0:T(8,128)(2,1)}, bf16[784,1024]{1,0:T(8,128)(2,1)S(1)}, u32[]{:S(2)}) copy-start(bf16[784,1024]{1,0:T(8,128)(2,1)S(1)} %get-tuple-element.166) | copy-start | bytes 4816900
  561.7 17.8 %slice-start.6 = ((s8[8388608]{0:T(1024)(128)(4,1)}), s8[4194304]{0:T(1024)(128)(4,1)S(1)}, s32[]{:S(2)}) async-start(s8[8388608]{0:T(1024)(128)(4,1)} %bitcast.286), calls=%async_computation.32 | async-start | bytes 8388608
  579.5 11.1 copy-start.12
  579.5 11.1 copy-start.15
  595.1 18.9 %copy-start.9 = (f32[784,1024]{1,0:T(8,128)}, f32[784,1024]{1,0:T(8,128)S(1)}, u32[]{:S(2)}) copy-start(f32[784,1024]{1,0:T(8,128)S(1)} %get-tuple-element.168) | copy-start | bytes 9633796
  598.9 399.7 %reduce-scatter.14.cloned.1.call-start = ((), (), s32[]{:S(2)}) async-start(), calls=%async_computation.21 | async-start | bytes 10485760 | tf_op jit(solution)/shard_map/reduce_scatter | solution.py:205
  618.7 79.8 %all-to-all-start.1 = ((bf16[784,4,256]{2,0,1:T(8,128)(2,1)}), bf16[784,4,256]{2,0,1:T(8,128)(2,1)S(1)}, u32[]{:S(2)}, u32[]{:S(2)}) async-start(bf16[784,4,256]{2,0,1:T(8,128)(2,1)} %bitcast.170), calls=%async_computation.1 | async-start | bytes 3211264 | tf_op jit(solution)/shard_map/all_to_all | solution.py:226
  622.3 377.0 %reduce-scatter.18.cloned.1.call-start = ((), (), s32[]{:S(2)}) async-start(), calls=%async_computation.23 | async-start | bytes 10485760 | tf_op jit(solution)/shard_map/reduce_scatter | solution.py:208
  636.6 410.0 %reduce-scatter.12.cloned.1.call-start = ((), (), s32[]{:S(2)}) async-start(), calls=%async_computation.20 | async-start | bytes 786432 | tf_op jit(solution)/shard_map/reduce_scatter | solution.py:280
  726.9 57.0 %copy-start.3 = (bf16[1568,3,4,64]{0,3,2,1:T(8,128)(2,1)}, bf16[1568,3,4,64]{0,3,2,1:T(8,128)(2,1)S(1)}, u32[]{:S(2)}) copy-start(bf16[1568,3,4,64]{0,3,2,1:T(8,128)(2,1)S(1)} %dynamic-slice_bitcast_fusion.21) | copy-start | bytes 7225348 | tf_op jit(solution)/shard_map/while
  812.0 20.2 %slice-start = ((s8[20873216]{0:T(1024)(128)(4,1)}), s8[4194304]{0:T(1024)(128)(4,1)S(1)}, s32[]{:S(2)}) async-start(s8[20873216]{0:T(1024)(128)(4,1)} %bitcast.249), calls=%async_computation.26 | async-start | bytes 8388608 | tf_op jit(solution)/shard_map/while
  812.0 20.2 %slice-start.1 = ((s8[20873216]{0:T(1024)(128)(4,1)}), s8[4096000]{0:T(1024)(128)(4,1)S(1)}, s32[]{:S(2)}) async-start(s8[20873216]{0:T(1024)(128)(4,1)} %bitcast.249), calls=%async_computation.27 | async-start | bytes 8192000 | tf_op jit(solution)/shard_map/while
  818.4 13.8 %slice-start.2 = ((s8[20873216]{0:T(1024)(128)(4,1)}), s8[4194304]{0:T(1024)(128)(4,1)S(1)}, s32[]{:S(2)}) async-start(s8[20873216]{0:T(1024)(128)(4,1)} %bitcast.249), calls=%async_computation.28 | async-start | bytes 8388608 | tf_op jit(solution)/shard_map/while
  818.4 13.8 %slice-start.3 = ((s8[20873216]{0:T(1024)(128)(4,1)}), s8[4194304]{0:T(1024)(128)(4,1)S(1)}, s32[]{:S(2)}) async-start(s8[20873216]{0:T(1024)(128)(4,1)} %bitcast.249), calls=%async_computation.29 | async-start | bytes 8388608 | tf_op jit(solution)/shard_map/while
  848.1 57.5 %copy-start.3 = (bf16[1568,3,4,64]{0,3,2,1:T(8,128)(2,1)}, bf16[1568,3,4,64]{0,3,2,1:T(8,128)(2,1)S(1)}, u32[]{:S(2)}) copy-start(bf16[1568,3,4,64]{0,3,2,1:T(8,128)(2,1)S(1)} %dynamic-slice_bitcast_fusion.21) | copy-start | bytes 7225348 | tf_op jit(solution)/shard_map/while
  933.5 19.8 %slice-start = ((s8[20873216]{0:T(1024)(128)(4,1)}), s8[4194304]{0:T(1024)(128)(4,1)S(1)}, s32[]{:S(2)}) async-start(s8[20873216]{0:T(1024)(128)(4,1)} %bitcast.249), calls=%async_computation.26 | async-start | bytes 8388608 | tf_op jit(solution)/shard_map/while
  933.5 19.8 %slice-start.1 = ((s8[20873216]{0:T(1024)(128)(4,1)}), s8[4096000]{0:T(1024)(128)(4,1)S(1)}, s32[]{:S(2)}) async-start(s8[20873216]{0:T(1024)(128)(4,1)} %bitcast.249), calls=%async_computation.27 | async-start | bytes 8192000 | tf_op jit(solution)/shard_map/while
  939.9 13.4 slice-start.2
  939.9 13.4 slice-start.3
  988.4 58.2 %reduce-scatter.8.cloned.1.call-start = ((), (), s32[]{:S(2)}) async-start(), calls=%async_computation.18 | async-start | bytes 2359296 | tf_op jit(solution)/shard_map/reduce_scatter | solution.py:277
  998.5 48.2 %reduce-scatter.16.cloned.1.call-start = ((), (), s32[]{:S(2)}) async-start(), calls=%async_computation.22 | async-start | bytes 3145728 | tf_op jit(solution)/shard_map/reduce_scatter | solution.py:283
  999.3 47.4 %reduce-scatter.20.cloned.1.call-start = ((), (), s32[]{:S(2)}) async-start(), calls=%async_computation.24 | async-start | bytes 3145728 | tf_op jit(solution)/shard_map/reduce_scatter | solution.py:286
  999.8 299.6 %all-gather.23.cloned.1.call-start = ((), (), s32[]{:S(2)}) async-start(), calls=%async_computation.17 | async-start | bytes 7864320 | tf_op jit(solution)/shard_map/all_gather | solution.py:177
  1037.1 244.6 %all-to-all-start.2 = ((bf16[3136,3,256]{2,1,0:T(4,128)(2,1)}), bf16[3136,3,256]{2,1,0:T(4,128)(2,1)}, u32[]{:S(2)}, u32[]{:S(2)}) async-start(bf16[3136,3,256]{2,1,0:T(4,128)(2,1)} %reshape.166), calls=%async_computation.2 | async-start | bytes 12845056 | tf_op jit(solution)/shard_map/all_to_all | solution.py:240
  1042.4 321.2 %all-reduce.5.cloned.1.call-start = ((), (), s32[]{:S(2)}) async-start(), calls=%async_computation.25 | async-start | bytes 6291456 | tf_op jit(solution)/shard_map/psum | solution.py:291
  1289.8 9.6 copy-start.26
  1289.8 9.6 copy-start.28
  1299.5 10.6 copy-start.29
  1299.5 10.6 copy-start.32
  1299.5 10.5 copy-start.33
  1299.5 10.5 copy-start.34
  1299.5 10.6 copy-start.31
  (42 other events, 197.8 us)
Sparse Core Ops, SparseCore 0:
  9.6 13.2 all-gather.14
  24.5 11.7 all-gather.18
  38.4 10.9 all-gather.10
  51.4 118.6 all-gather.8
  171.5 44.1 all-gather.12
  217.1 182.7 all-gather.16
  401.5 147.7 all-gather.20
  599.0 55.8 reduce-scatter.9
  657.3 151.0 reduce-scatter.13
  810.7 145.4 reduce-scatter.17
  988.6 6.2 reduce-scatter.11
  998.6 9.1 reduce-scatter.7
  1010.1 10.8 reduce-scatter.15
  1023.0 10.7 reduce-scatter.19
  1035.4 229.2 all-gather.22
  1268.3 94.5 all-reduce.4
